TPU v7x, 512 devices: a whole 4x8x8 slice. The times are simulated.
512 devices in a mesh: occ: 64 (over x, y, core), aux: 8 (over z).
Axes of the slice: x: 4, y: 8, z: 8, core: 2. Of those that a mesh axis runs over, the one named last changes fastest.
Arguments:
- ao_blocks: bfloat16 [256, 256, 8192], P('occ', None, 'aux'), may hold values from -0.59765625 to 0.59765625
- pno_coef: bfloat16 [1024, 256, 200], P('occ'), may hold values from -0.375 to 0.375
- pno_energy: float32 [1024, 200], P('occ'), may hold values from 0.3 to 3
- occ_energy: float32 [256], replicated, may hold values from -1.5 to -0.3
- pair_partner: int32 [1024], P('occ'), may hold values from 0 to 255, as said below
- pno_count: int32 [1024], P('occ'), may hold values from 40 to 200, as said below
Outputs:
- amplitudes: float32 [1024, 200, 200], P(('occ', 'aux'))
- orbital_pair_energy: float32 [256], P('occ')
Inputs may be any that keep to these rules, and one draw needn't show every extreme that they name: pair_partner[s] differs from own(s) and is an orbital owned by the same index of occ as own(s), or by the index just below or just above it. `pno_count`: every count is a multiple of 8; in every block of 16 pairs one count is 200 and one is 40.
All inputs are finite; a program needn't handle non-finite values.
Results may differ from a plain program's by a relative error of at most 0.0041.
Values may be sent and summed in bfloat16 or wider, within the bound.
A program may use at most 128 MiB of HBM per device.

v0:
```python
import jax
import jax.numpy as jnp
from jax import lax
from jax.sharding import PartitionSpec as P


def padded(cells, sides, width):
    for axis, dim in sides:
        count = lax.axis_size(axis)
        ends = count - 1
        head = lax.slice_in_dim(cells, 0, width, axis=dim)
        tail = lax.slice_in_dim(cells, cells.shape[dim] - width, cells.shape[dim], axis=dim)
        cells = jnp.concatenate(
            [
                lax.ppermute(tail, axis, [(i, (i + 1) % count) for i in range(ends)]),
                cells,
                lax.ppermute(head, axis, [((i + 1) % count, i) for i in range(ends)]),
            ],
            axis=dim,
        )
    return cells


def shards(ao_blocks, pno_coef, pno_energy, occ_energy, pair_partner, pno_count):
    orb_dev = ao_blocks.shape[0]
    virtuals = ao_blocks.shape[1]
    aux_block = ao_blocks.shape[2]
    pair_dev = pno_coef.shape[0]
    pno_max = pno_coef.shape[2]
    per_orbital = pair_dev // orb_dev
    occ_place = lax.axis_index("occ")
    aux_place = lax.axis_index("aux")
    columns = jnp.arange(pno_max, dtype=jnp.int32)
    kept_mask = (columns[None, :] < pno_count[:, None]).astype(jnp.bfloat16)
    masked_coef = pno_coef * kept_mask[:, None, :]
    projected_own = (
        jnp.einsum(
            "ornp,onk->orpk",
            masked_coef.reshape(orb_dev, per_orbital, virtuals, pno_max),
            ao_blocks,
            preferred_element_type=jnp.float32,
        )
        .astype(jnp.bfloat16)
        .reshape(pair_dev, pno_max, aux_block)
    )
    nearby = padded(ao_blocks, (("occ", 0),), orb_dev)
    window_slot = pair_partner - (occ_place - 1) * orb_dev
    partner_blocks = jnp.take(nearby, window_slot, axis=0)
    projected_partner = jnp.einsum(
        "snp,snk->spk", masked_coef, partner_blocks, preferred_element_type=jnp.float32
    ).astype(jnp.bfloat16)
    partials = jnp.einsum(
        "spk,sqk->spq", projected_own, projected_partner, preferred_element_type=jnp.float32
    )
    share_rows = pair_dev // lax.axis_size("aux")
    first_row = aux_place * share_rows
    totals = lax.psum(partials, "aux")
    exchange_ints = lax.dynamic_slice_in_dim(totals, first_row, share_rows, 0)
    own_orbital = occ_place * orb_dev + jnp.arange(pair_dev, dtype=jnp.int32) // per_orbital
    mine_owner = lax.dynamic_slice_in_dim(own_orbital, first_row, share_rows, 0)
    mine_partner = lax.dynamic_slice_in_dim(pair_partner, first_row, share_rows, 0)
    energies = lax.dynamic_slice_in_dim(pno_energy, first_row, share_rows, 0)
    shift_occ = occ_energy[mine_owner] + occ_energy[mine_partner]
    denominator = energies[:, :, None] + energies[:, None, :] - shift_occ[:, None, None]
    amplitudes = -exchange_ints / denominator
    pair_energy = jnp.sum(
        (2.0 * exchange_ints - jnp.swapaxes(exchange_ints, 1, 2)) * amplitudes, axis=(1, 2)
    )
    half_energy = 0.5 * pair_energy
    orbital_ids = jnp.arange(occ_energy.shape[0], dtype=jnp.int32)
    hits = (orbital_ids[None, :] == mine_owner[:, None]).astype(jnp.float32) + (
        orbital_ids[None, :] == mine_partner[:, None]
    ).astype(jnp.float32)
    spread = jnp.sum(hits * half_energy[:, None], axis=0)
    whole_sum = lax.psum(spread, ("occ", "aux"))
    orbital = lax.dynamic_slice_in_dim(whole_sum, occ_place * orb_dev, orb_dev, 0)
    return (amplitudes, orbital)


def solution(mesh):
    return jax.shard_map(
        shards,
        mesh=mesh,
        in_specs=(
            P("occ", None, "aux"),
            P("occ", None, None),
            P("occ", None),
            P(),
            P("occ"),
            P("occ"),
        ),
        out_specs=(P(("occ", "aux"), None, None), P("occ")),
        check_vma=False,
    )
```

profile of v0, /device:TPU:1, one launch (start us, length us, event | category | flops | bytes accessed | tf_op | source)
XLA Modules:
  0.0 275.3 jit_solution(15171100014383080903)
XLA Ops:
  7.2 0.0 copy-start
  7.2 0.0 copy-start.2
  7.2 0.0 all-reduce.2.cloned.1.call-start
  7.2 4.7 %collective-permute-start = (bf16[4,256,1024]{2,1,0:T(8,128)(2,1)}, bf16[4,256,1024]{2,1,0:T(8,128)(2,1)}, u32[]{:S(2)}, u32[]{:S(2)}) collective-permute-start(bf16[4,256,1024]{2,1,0:T(8,128)(2,1)} %param.6), channel_id=1, source_target_pairs={{0,8},{8,16},{16,24},{24,32},{32,40},{40,48},{48,56},{56,64},{64,7... | collective-permute-start | bytes 6291464 | tf_op jit(solution)/shard_map/ppermute | solution.py:15
  12.0 6.8 %collective-permute-start.1 = (bf16[4,256,1024]{2,1,0:T(8,128)(2,1)}, bf16[4,256,1024]{2,1,0:T(8,128)(2,1)}, u32[]{:S(2)}, u32[]{:S(2)}) collective-permute-start(bf16[4,256,1024]{2,1,0:T(8,128)(2,1)} %param.6), channel_id=1, source_target_pairs={{8,0},{16,8},{24,16},{32,24},{40,32},{48,40},{56,48},{64,56},{72,6... | collective-permute-start | bytes 6291464 | tf_op jit(solution)/shard_map/ppermute | solution.py:17
  18.7 0.7 compare_and_fusion
  19.4 0.7 fusion.13
  20.1 1.9 broadcast_multiply_fusion
  22.0 0.0 copy-start.3
  22.1 0.0 copy-done.2
  22.1 4.7 %convolution_convert_fusion = bf16[4,4,200,1024]{3,2,1,0:T(8,128)(2,1)} fusion(bf16[4,4,256,200]{2,3,1,0:T(8,128)(2,1)S(1)} %bitcast.16, bf16[4,256,1024]{2,1,0:T(8,128)(2,1)S(1)} %copy-done.2), kind=kOutput, calls=%fused_computation.8 | convolution fusion | flops 1680998400 | bytes 10289152 | tf_op jit(solution)/shard_map/ornp,onk->orpk/dot_general | solution.py:37
  26.8 0.0 copy-done.3
  26.8 8.5 %collective-permute-done = bf16[4,256,1024]{2,1,0:T(8,128)(2,1)} collective-permute-done((bf16[4,256,1024]{2,1,0:T(8,128)(2,1)}, bf16[4,256,1024]{2,1,0:T(8,128)(2,1)}, u32[]{:S(2)}, u32[]{:S(2)}) %collective-permute-start) | collective-permute-done | bytes 2097184 | tf_op jit(solution)/shard_map/ppermute | solution.py:15
  35.2 4.4 %collective-permute-done.1 = bf16[4,256,1024]{2,1,0:T(8,128)(2,1)} collective-permute-done((bf16[4,256,1024]{2,1,0:T(8,128)(2,1)}, bf16[4,256,1024]{2,1,0:T(8,128)(2,1)}, u32[]{:S(2)}, u32[]{:S(2)}) %collective-permute-start.1) | collective-permute-done | bytes 2097184 | tf_op jit(solution)/shard_map/ppermute | solution.py:17
  39.6 5.5 %pad_maximum_fusion = bf16[12,256,1024]{2,1,0:T(8,128)(2,1)} fusion(bf16[4,256,1024]{2,1,0:T(8,128)(2,1)} %collective-permute-done.1, bf16[4,256,1024]{2,1,0:T(8,128)(2,1)S(1)} %copy-done.2, bf16[4,256,1024]{2,1,0:T(8,128)(2,1)} %collective-permute-done), kind=kLoop, calls=%fused_computation.7 | loop fusion | flops 6291456 | bytes 12582912 | tf_op jit(solution)/shard_map/concatenate | solution.py:13
  45.1 0.0 copy-start.4
  45.1 7.7 %gather_fusion = bf16[16,256,1024]{2,1,0:T(8,128)(2,1)} fusion(bf16[12,256,1024]{2,1,0:T(8,128)(2,1)} %pad_maximum_fusion, s32[1024]{0:T(1024)S(1)} %pad_clamp_fusion.2), kind=kCustom, calls=%fused_computation | custom fusion | bytes 16777280 | tf_op jit(solution)/shard_map/jit(_take)/gather | solution.py:48
  52.8 0.0 copy-done.4
  52.8 0.0 copy-start.5
  52.8 0.0 copy-start.1
  52.8 10.8 %fusion.9 = f32[16,200,200]{2,1,0:T(8,128)} fusion(bf16[16,200,1024]{2,1,0:T(8,128)(2,1)} %bitcast.17, bf16[16,256,200]{1,2,0:T(8,128)(2,1)S(1)} %copy-done.4, bf16[16,256,1024]{2,1,0:T(8,128)(2,1)} %gather_fusion, pred[16]{0:T(512)(128)(4,1)S(1)} %get-tuple-element.12), kind=kOutput, calls=%fused_computation.11 | convolution fusion | flops 2995912704 | bytes 19140624 | tf_op jit(solution)/shard_map/spk,sqk->spq/dot_general | solution.py:52
  63.6 0.0 all-reduce.2.cloned.1.call-update
  63.6 0.0 copy-done.5
  63.6 0.1 compare_select_fusion
  63.7 0.0 copy-done.1
  63.7 0.6 gather_fusion.1
  64.3 0.6 gather_fusion.2
  65.0 0.0 copy-done
  65.0 102.3 %all-reduce.2.cloned.1.call-done = f32[16,200,200]{2,1,0:T(8,128)} async-done(((f32[16,200,200]{2,1,0:T(8,128)}), f32[16,200,200]{2,1,0:T(8,128)}) %all-reduce.2.cloned.1.call-update) | async-done | bytes 2560016 | tf_op jit(solution)/shard_map/psum | solution.py:57
  167.3 1.0 constant_dynamic-slice_fusion.1
  168.3 0.2 copy.14
  168.5 1.3 fusion.12
  169.8 0.9 copy.16
  170.8 0.1 fusion.16
  170.8 97.1 %psum.15 = f32[256]{0:T(256)S(1)} all-reduce(f32[256]{0:T(256)S(1)} %fusion.16), channel_id=1, replica_groups=mesh['occ'=64,'aux'=8] {'occ','aux'}, use_global_device_ids=true, to_apply=%region_3.4 | all-reduce | flops 256 | bytes 2048 | tf_op jit(solution)/shard_map/psum | solution.py:75
  267.9 0.6 dynamic_slice.19
  (7 shorter events, 0.0 us)
Async XLA Ops:
  7.2 57.8 %copy-start = (f32[16,200]{1,0:T(8,128)S(1)}, f32[16,200]{1,0:T(8,128)}, u32[]{:S(2)}) copy-start(f32[16,200]{1,0:T(8,128)} %param.8) | copy-start | bytes 38404
  7.2 14.9 %copy-start.2 = (bf16[4,256,1024]{2,1,0:T(8,128)(2,1)S(1)}, bf16[4,256,1024]{2,1,0:T(8,128)(2,1)}, u32[]{:S(2)}) copy-start(bf16[4,256,1024]{2,1,0:T(8,128)(2,1)} %param.6) | copy-start | bytes 6291460
  7.2 160.1 %all-reduce.2.cloned.1.call-start = ((), (), s32[]{:S(2)}) async-start(), calls=%async_computation | async-start | bytes 6553600 | tf_op jit(solution)/shard_map/psum | solution.py:57
  7.2 28.0 %collective-permute-start = (bf16[4,256,1024]{2,1,0:T(8,128)(2,1)}, bf16[4,256,1024]{2,1,0:T(8,128)(2,1)}, u32[]{:S(2)}, u32[]{:S(2)}) collective-permute-start(bf16[4,256,1024]{2,1,0:T(8,128)(2,1)} %param.6), channel_id=1, source_target_pairs={{0,8},{8,16},{16,24},{24,32},{32,40},{40,48},{48,56},{56,64},{64,7... | collective-permute-start | bytes 6291464 | tf_op jit(solution)/shard_map/ppermute | solution.py:15
  12.0 27.7 %collective-permute-start.1 = (bf16[4,256,1024]{2,1,0:T(8,128)(2,1)}, bf16[4,256,1024]{2,1,0:T(8,128)(2,1)}, u32[]{:S(2)}, u32[]{:S(2)}) collective-permute-start(bf16[4,256,1024]{2,1,0:T(8,128)(2,1)} %param.6), channel_id=1, source_target_pairs={{8,0},{16,8},{24,16},{32,24},{40,32},{48,40},{56,48},{64,56},{72,6... | collective-permute-start | bytes 6291464 | tf_op jit(solution)/shard_map/ppermute | solution.py:17
  22.0 4.7 %copy-start.3 = (bf16[16,256,200]{1,2,0:T(8,128)(2,1)}, bf16[16,256,200]{1,2,0:T(8,128)(2,1)S(1)}, u32[]{:S(2)}) copy-start(bf16[16,256,200]{1,2,0:T(8,128)(2,1)S(1)} %broadcast_multiply_fusion) | copy-start | bytes 4915204
  45.1 7.7 %copy-start.4 = (bf16[16,256,200]{1,2,0:T(8,128)(2,1)S(1)}, bf16[16,256,200]{1,2,0:T(8,128)(2,1)}, u32[]{:S(2)}) copy-start(bf16[16,256,200]{1,2,0:T(8,128)(2,1)} %copy-done.3) | copy-start | bytes 4915204
  52.8 10.8 %copy-start.5 = (s32[16]{0:T(128)S(1)}, s32[16]{0:T(128)}, u32[]{:S(2)}) copy-start(s32[16]{0:T(128)} %param.10) | copy-start | bytes 196
  52.8 10.9 %copy-start.1 = (f32[256]{0:T(256)S(1)}, f32[256]{0:T(256)}, u32[]{:S(2)}) copy-start(f32[256]{0:T(256)} %param.9) | copy-start | bytes 3076
Sparse Core Ops, SparseCore 0:
  63.7 103.5 all-reduce.1
where the time goes:
time: 276 us; the launch traced here: 275 us
  waiting for transfers between devices  115 us (42%)
  blocking collectives  97.1 us (35%)
  matrix products  15.4 us (6%)
  between operations  14.1 us (5%)
  local copies, waits for them, and re-layouts  11.7 us (4%)
  starting transfers between devices  11.5 us (4%)
  other arithmetic  10.3 us (4%)
    psum x1, waiting for transfers between devices, shards(): totals = lax.psum(partials, 'aux')  102 us
    psum x1, blocking collectives, shards(): whole_sum = lax.psum(spread, ('occ', 'aux'))  97.1 us
    dot_general x1, matrix products, shards(): jnp.einsum('spk,sqk->spq', projected_own, projected_partner, preferred_el...  10.8 us
    ppermute x1, waiting for transfers between devices, padded(): lax.ppermute(tail, axis, [(i, (i + 1) % count) for i in range(ends)])  8.47 us
    gather x1, local copies, waits for them, and re-layouts, shards(): partner_blocks = jnp.take(nearby, window_slot, axis=0)  7.67 us
    ppermute x1, starting transfers between devices, padded(): lax.ppermute(head, axis, [((i + 1) % count, i) for i in range(ends)])  6.75 us
  transfers between devices with their start and end apart: 3, of which 3 were waited for; matrix products, arithmetic and copies ran while one was open for 3% of the time, Pallas kernels for 0%

commit v1 on v0

--- a/solution.py
+++ b/solution.py
@@ -54,7 +54,7 @@
     )
     share_rows = pair_dev // lax.axis_size("aux")
     first_row = aux_place * share_rows
-    totals = lax.psum(partials, "aux")
+    totals = jnp.sum(lax.all_gather(partials, "aux"), axis=0)
     exchange_ints = lax.dynamic_slice_in_dim(totals, first_row, share_rows, 0)
     own_orbital = occ_place * orb_dev + jnp.arange(pair_dev, dtype=jnp.int32) // per_orbital
     mine_owner = lax.dynamic_slice_in_dim(own_orbital, first_row, share_rows, 0)

time: 276 us -> 454 us (1.64)
  waiting for transfers between devices: 115 us -> 279 us
  other arithmetic: 10.3 us -> 21.7 us
    all_gather x0 -> x1, waiting for transfers between devices: none -> 265 us  [shards(): totals = jnp.sum(lax.all_gather(partials, 'aux'), axis=0)]
    psum x1 -> x0, waiting for transfers between devices: 102 us -> none  [shards(): totals = lax.psum(partials, 'aux')]
    reduce_sum x0 -> x1, other arithmetic: none -> 10.6 us  [shards(): totals = jnp.sum(lax.all_gather(partials, 'aux'), axis=0)]
  transfers between devices with their start and end apart: 3 -> 3, of which waited for: 3 -> 3; matrix products, arithmetic and copies ran while one was open for 3% -> 2% of each run, Pallas kernels for 0% -> 0%
where the time goes in v1:
time: 454 us
  waiting for transfers between devices  279 us (61%)
  blocking collectives  97.1 us (21%)
  other arithmetic  21.7 us (5%)
  matrix products  17 us (4%)
  local copies, waits for them, and re-layouts  14.1 us (3%)
  between operations  14.1 us (3%)
  starting transfers between devices  10.7 us (2%)
    all_gather x1, waiting for transfers between devices, shards(): totals = jnp.sum(lax.all_gather(partials, 'aux'), axis=0)  265 us
    psum x1, blocking collectives, shards(): whole_sum = lax.psum(spread, ('occ', 'aux'))  97.1 us
    dot_general x1, matrix products, shards(): jnp.einsum('spk,sqk->spq', projected_own, projected_partner, preferred_el...  10.8 us
    reduce_sum x1, other arithmetic, shards(): totals = jnp.sum(lax.all_gather(partials, 'aux'), axis=0)  10.6 us
  transfers between devices with their start and end apart: 3, of which 3 were waited for; matrix products, arithmetic and copies ran while one was open for 2% of the time, Pallas kernels for 0%

profile of v1, /device:TPU:1, one launch (start us, length us, event | category | flops | bytes accessed | tf_op | source)
XLA Modules:
  0.0 453.7 jit_solution(16637419878309475972)
XLA Ops:
  7.2 0.0 copy-start
  7.2 0.0 all-gather.3.cloned.1.call-start
  7.2 8.8 %collective-permute-start.1 = (bf16[4,256,1024]{2,1,0:T(8,128)(2,1)}, bf16[4,256,1024]{2,1,0:T(8,128)(2,1)}, u32[]{:S(2)}, u32[]{:S(2)}) collective-permute-start(bf16[4,256,1024]{2,1,0:T(8,128)(2,1)} %param.6), channel_id=1, source_target_pairs={{8,0},{16,8},{24,16},{32,24},{40,32},{48,40},{56,48},{64,56},{72,6... | collective-permute-start | bytes 6291464 | tf_op jit(solution)/shard_map/ppermute | solution.py:17
  16.0 1.9 collective-permute-start
  17.9 0.7 compare_and_fusion
  18.6 0.7 fusion.13
  19.3 0.0 copy-start.2
  19.3 2.1 broadcast_multiply_fusion
  21.4 6.3 %convolution_convert_fusion = bf16[4,4,200,1024]{3,2,1,0:T(8,128)(2,1)} fusion(bf16[4,4,256,200]{2,3,1,0:T(8,128)(2,1)S(1)} %bitcast.18, bf16[4,256,1024]{2,1,0:T(8,128)(2,1)} %param.6), kind=kOutput, calls=%fused_computation.8 | convolution fusion | flops 1680998400 | bytes 10289152 | tf_op jit(solution)/shard_map/ornp,onk->orpk/dot_general | solution.py:37
  27.7 8.2 %collective-permute-done.1 = bf16[4,256,1024]{2,1,0:T(8,128)(2,1)} collective-permute-done((bf16[4,256,1024]{2,1,0:T(8,128)(2,1)}, bf16[4,256,1024]{2,1,0:T(8,128)(2,1)}, u32[]{:S(2)}, u32[]{:S(2)}) %collective-permute-start.1) | collective-permute-done | bytes 2097184 | tf_op jit(solution)/shard_map/ppermute | solution.py:17
  35.8 5.3 %collective-permute-done = bf16[4,256,1024]{2,1,0:T(8,128)(2,1)} collective-permute-done((bf16[4,256,1024]{2,1,0:T(8,128)(2,1)}, bf16[4,256,1024]{2,1,0:T(8,128)(2,1)}, u32[]{:S(2)}, u32[]{:S(2)}) %collective-permute-start) | collective-permute-done | bytes 2097184 | tf_op jit(solution)/shard_map/ppermute | solution.py:15
  41.2 0.0 copy-done.2
  41.2 5.5 %pad_maximum_fusion = bf16[12,256,1024]{2,1,0:T(8,128)(2,1)} fusion(bf16[4,256,1024]{2,1,0:T(8,128)(2,1)} %collective-permute-done.1, bf16[4,256,1024]{2,1,0:T(8,128)(2,1)S(1)} %copy-done.2, bf16[4,256,1024]{2,1,0:T(8,128)(2,1)} %collective-permute-done), kind=kLoop, calls=%fused_computation.7 | loop fusion | flops 6291456 | bytes 12582912 | tf_op jit(solution)/shard_map/concatenate | solution.py:13
  46.7 7.5 %gather_fusion = bf16[16,256,1024]{2,1,0:T(8,128)(2,1)} fusion(bf16[12,256,1024]{2,1,0:T(8,128)(2,1)} %pad_maximum_fusion, s32[1024]{0:T(1024)S(1)} %pad_clamp_fusion.2), kind=kCustom, calls=%fused_computation | custom fusion | bytes 16777280 | tf_op jit(solution)/shard_map/jit(_take)/gather | solution.py:48
  54.2 0.0 copy-start.3
  54.2 0.0 copy-start.1
  54.2 10.8 %fusion.9 = f32[16,200,200]{2,1,0:T(8,128)} fusion(bf16[16,200,1024]{2,1,0:T(8,128)(2,1)} %bitcast.19, bf16[16,256,200]{1,2,0:T(8,128)(2,1)S(1)} %broadcast_multiply_fusion, bf16[16,256,1024]{2,1,0:T(8,128)(2,1)} %gather_fusion, pred[16]{0:T(512)(128)(4,1)S(1)} %get-tuple-element.10), kind=kOutput, calls=%fused_computation.11 | convolution fusion | flops 2995912704 | bytes 19140624 | tf_op jit(solution)/shard_map/spk,sqk->spq/dot_general | solution.py:52
  65.0 0.0 all-gather.3.cloned.1.call-update
  65.0 0.0 copy-done.3
  65.0 0.1 compare_select_fusion
  65.1 0.0 copy-done.1
  65.1 0.6 gather_fusion.1
  65.8 0.6 gather_fusion.2
  66.4 0.0 copy-done
  66.4 265.5 %all-gather.3.cloned.1.call-done = f32[128,200,200]{2,1,0:T(8,128)} async-done(((f32[16,200,200]{2,1,0:T(8,128)}), f32[128,200,200]{2,1,0:T(8,128)}) %all-gather.3.cloned.1.call-update) | async-done | bytes 20480016 | tf_op jit(solution)/shard_map/all_gather | solution.py:57
  331.9 10.6 %reduce_sum.27 = f32[16,200,200]{2,1,0:T(8,128)S(1)} reduce(f32[8,16,200,200]{3,2,1,0:T(8,128)} %bitcast.17, f32[]{:T(128)} %constant.50.clone.1), dimensions={0}, to_apply=%region_0.1 | reduce | flops 4480000 | bytes 23040004 | tf_op jit(solution)/shard_map/reduce_sum | solution.py:57
  342.5 0.8 constant_dynamic-slice_fusion.1
  343.3 1.9 copy.15
  345.2 1.9 fusion.12
  347.2 1.9 copy.17
  349.1 0.1 fusion.16
  349.2 97.1 %psum.7 = f32[256]{0:T(256)S(1)} all-reduce(f32[256]{0:T(256)S(1)} %fusion.16), channel_id=1, replica_groups=mesh['occ'=64,'aux'=8] {'occ','aux'}, use_global_device_ids=true, to_apply=%region_3.4 | all-reduce | flops 256 | bytes 2048 | tf_op jit(solution)/shard_map/psum | solution.py:75
  446.3 0.6 dynamic_slice.19
  (7 shorter events, 0.0 us)
Async XLA Ops:
  7.2 59.3 %copy-start = (f32[16,200]{1,0:T(8,128)S(1)}, f32[16,200]{1,0:T(8,128)}, u32[]{:S(2)}) copy-start(f32[16,200]{1,0:T(8,128)} %param.8) | copy-start | bytes 38404
  7.2 324.7 %all-gather.3.cloned.1.call-start = ((), (), s32[]{:S(2)}) async-start(), calls=%async_computation | async-start | bytes 29491200 | tf_op jit(solution)/shard_map/all_gather | solution.py:57
  7.2 28.6 %collective-permute-start.1 = (bf16[4,256,1024]{2,1,0:T(8,128)(2,1)}, bf16[4,256,1024]{2,1,0:T(8,128)(2,1)}, u32[]{:S(2)}, u32[]{:S(2)}) collective-permute-start(bf16[4,256,1024]{2,1,0:T(8,128)(2,1)} %param.6), channel_id=1, source_target_pairs={{8,0},{16,8},{24,16},{32,24},{40,32},{48,40},{56,48},{64,56},{72,6... | collective-permute-start | bytes 6291464 | tf_op jit(solution)/shard_map/ppermute | solution.py:17
  16.0 25.2 %collective-permute-start = (bf16[4,256,1024]{2,1,0:T(8,128)(2,1)}, bf16[4,256,1024]{2,1,0:T(8,128)(2,1)}, u32[]{:S(2)}, u32[]{:S(2)}) collective-permute-start(bf16[4,256,1024]{2,1,0:T(8,128)(2,1)} %param.6), channel_id=1, source_target_pairs={{0,8},{8,16},{16,24},{24,32},{32,40},{40,48},{48,56},{56,64},{64,7... | collective-permute-start | bytes 6291464 | tf_op jit(solution)/shard_map/ppermute | solution.py:15
  19.3 21.9 %copy-start.2 = (bf16[4,256,1024]{2,1,0:T(8,128)(2,1)S(1)}, bf16[4,256,1024]{2,1,0:T(8,128)(2,1)}, u32[]{:S(2)}) copy-start(bf16[4,256,1024]{2,1,0:T(8,128)(2,1)} %param.6) | copy-start | bytes 6291460
  54.2 10.8 %copy-start.3 = (s32[16]{0:T(128)S(1)}, s32[16]{0:T(128)}, u32[]{:S(2)}) copy-start(s32[16]{0:T(128)} %param.10) | copy-start | bytes 196
  54.2 10.9 %copy-start.1 = (f32[256]{0:T(256)S(1)}, f32[256]{0:T(256)}, u32[]{:S(2)}) copy-start(f32[256]{0:T(256)} %param.9) | copy-start | bytes 3076
Sparse Core Ops, SparseCore 0:
  65.1 266.7 all-gather.2
